TPU v7x, 32 devices: a whole 2x2x4 slice. The times are simulated.
32 devices in a mesh: rep: 8 (over z, core), fsdp: 4 (over y, x).
Axes of the slice: x: 2, y: 2, z: 4, core: 2. Of those that a mesh axis runs over, the one named last changes fastest.
Arguments:
- hidden_in: bfloat16 [10240, 1536], P(('rep', 'fsdp')), may hold values from -6 to 6
- out_grad: bfloat16 [10240, 1536], P(('rep', 'fsdp')), may hold values from -6 to 6
- doc_lengths: int32 [8, 8], P('rep'), may hold values from 1 to 1024, 1280 in all within a row
- piece_starts: int32 [8, 2], P('rep'), may hold values from 0 to 1024, as said below
- w_query: bfloat16 [1536, 1536], P('fsdp'), may hold values from -0.15625 to 0.15625
- b_query: bfloat16 [1536], P('fsdp'), may hold values from -3 to 3
- w_key: bfloat16 [1536, 256], P('fsdp'), may hold values from -0.15625 to 0.15625
- b_key: bfloat16 [256], P('fsdp'), may hold values from -3 to 3
- w_value: bfloat16 [1536, 256], P('fsdp'), may hold values from -0.15625 to 0.15625
- b_value: bfloat16 [256], P('fsdp'), may hold values from -3 to 3
- w_output: bfloat16 [1536, 1536], P('fsdp'), may hold values from -0.625 to 0.625
- gain_attn: bfloat16 [1536], P('fsdp'), may hold values from 0.5 to 1.5
- w_gate: bfloat16 [1536, 8960], P('fsdp'), may hold values from -0.15625 to 0.15625
- w_up: bfloat16 [1536, 8960], P('fsdp'), may hold values from -0.15625 to 0.15625
- w_down: bfloat16 [8960, 1536], P('fsdp'), may hold values from -0.0625 to 0.0625
- gain_mlp: bfloat16 [1536], P('fsdp'), may hold values from 0.5 to 1.5
Outputs:
- output: float32 [10240, 1536], P(('rep', 'fsdp'))
- grad_input: float32 [10240, 1536], P(('rep', 'fsdp'))
- grad_w_query: float32 [1536, 1536], P('fsdp')
- grad_b_query: float32 [1536], P('fsdp')
- grad_w_key: float32 [1536, 256], P('fsdp')
- grad_b_key: float32 [256], P('fsdp')
- grad_w_value: float32 [1536, 256], P('fsdp')
- grad_b_value: float32 [256], P('fsdp')
- grad_w_output: float32 [1536, 1536], P('fsdp')
- grad_gain_attn: float32 [1536], P('fsdp')
- grad_w_gate: float32 [1536, 8960], P('fsdp')
- grad_w_up: float32 [1536, 8960], P('fsdp')
- grad_w_down: float32 [8960, 1536], P('fsdp')
- grad_gain_mlp: float32 [1536], P('fsdp')
Inputs may be any that keep to these rules, and one draw needn't show every extreme that they name: `doc_lengths`: each row's 8 lengths sum to 1280, and the longest is exactly 1024. `piece_starts`: in each row the starts rise by 256 or more from piece to piece, so pieces never intersect; a piece may run over a document's end.
All inputs are finite; a program needn't handle non-finite values.
Results may differ from a plain program's by a relative error of at most 0.028.
Values may be sent and summed in bfloat16 or wider, within the bound.
A program may use at most 576 MiB of HBM per device.

v0:
```python
import jax
import jax.numpy as jnp
from jax import lax
from jax.sharding import PartitionSpec as P

HEADS = 12
KVH = 2
HDIM = 128
PIECE = 256
epsilon = 1e-06
rope_base = 1000000.0


def row_layout(positions, lengths, starts, piece_len):
    doc_ends = jnp.cumsum(lengths)
    passed = positions[:, None] >= doc_ends[None, :]
    doc_ids = jnp.sum(passed.astype(jnp.int32), axis=1, dtype=jnp.int32)
    offsets = jnp.sum(jnp.where(passed, lengths[None, :], 0), axis=1, dtype=jnp.int32)
    inside = (positions[:, None] >= starts[None, :]) & (
        positions[:, None] < starts[None, :] + piece_len
    )
    labels = jnp.arange(1, starts.shape[0] + 1, dtype=jnp.int32)
    piece_ids = jnp.sum(jnp.where(inside, labels[None, :], 0), axis=1, dtype=jnp.int32)
    return (doc_ids, positions - offsets, piece_ids)


def visible_pairs(query_doc, query_pos, query_piece, key_doc, key_pos, key_piece):
    same_doc = query_doc[:, None] == key_doc[None, :]
    causal = key_pos[None, :] <= query_pos[:, None]
    same_piece = (query_piece[:, None] == key_piece[None, :]) & (query_piece[:, None] > 0)
    return same_doc & (causal | same_piece)


def rope_tables(relative, head_dim):
    halves = jnp.arange(0, head_dim, 2).astype(jnp.float32) / head_dim
    inverse = rope_base ** (-halves)
    angles = relative.astype(jnp.float32)[:, None] * inverse[None, :]
    angles = jnp.concatenate([angles, angles], axis=1)
    return (jnp.cos(angles), jnp.sin(angles))


def rotate(values, cosine, sine):
    half_dim = values.shape[-1] // 2
    turned = jnp.concatenate([-values[..., half_dim:], values[..., :half_dim]], axis=-1)
    return values * cosine[:, None, :] + turned * sine[:, None, :]


def unrotate(grads, cosine, sine):
    half_dim = grads.shape[-1] // 2
    spun = grads * sine[:, None, :]
    turned_back = jnp.concatenate([spun[..., half_dim:], -spun[..., :half_dim]], axis=-1)
    return grads * cosine[:, None, :] + turned_back


def mat_dot(left, right):
    return jnp.dot(left, right, preferred_element_type=jnp.float32)


def dot_right_t(left, right):
    return lax.dot_general(
        left, right, (((1,), (1,)), ((), ())), preferred_element_type=jnp.float32
    )


def dot_left_t(left, right):
    return lax.dot_general(
        left, right, (((0,), (0,)), ((), ())), preferred_element_type=jnp.float32
    )


def local(
    hidden_in,
    out_grad,
    doc_lengths,
    piece_starts,
    w_query,
    b_query,
    w_key,
    b_key,
    w_value,
    b_value,
    w_output,
    gain_attn,
    w_gate,
    w_up,
    w_down,
    gain_mlp,
):
    tok_rows = hidden_in.shape[0]
    model_width = hidden_in.shape[1]
    shard_count = lax.axis_size("fsdp")
    row_len = tok_rows * shard_count
    group_size = HEADS // KVH
    kv_width = KVH * HDIM
    ff_width = w_gate.shape[1]
    score_scale = 1.0 / HDIM**0.5
    local_pos = lax.axis_index("fsdp") * tok_rows + jnp.arange(tok_rows, dtype=jnp.int32)
    row_pos = jnp.arange(row_len, dtype=jnp.int32)
    lengths = doc_lengths[0]
    starts = piece_starts[0]
    query_doc, query_rel, query_piece = row_layout(local_pos, lengths, starts, PIECE)
    key_doc, unused_rel, key_piece = row_layout(row_pos, lengths, starts, PIECE)
    allowed = visible_pairs(query_doc, local_pos, query_piece, key_doc, row_pos, key_piece)
    cosine, sine = rope_tables(query_rel, HDIM)
    (
        query_full,
        key_full,
        value_full,
        output_full,
        query_bias,
        key_bias,
        value_bias,
        attn_gain,
        mlp_gain,
    ) = (
        lax.all_gather(w_query, "fsdp", axis=0, tiled=True),
        lax.all_gather(w_key, "fsdp", axis=0, tiled=True),
        lax.all_gather(w_value, "fsdp", axis=0, tiled=True),
        lax.all_gather(w_output, "fsdp", axis=0, tiled=True),
        lax.all_gather(b_query, "fsdp", axis=0, tiled=True),
        lax.all_gather(b_key, "fsdp", axis=0, tiled=True),
        lax.all_gather(b_value, "fsdp", axis=0, tiled=True),
        lax.all_gather(gain_attn, "fsdp", axis=0, tiled=True),
        lax.all_gather(gain_mlp, "fsdp", axis=0, tiled=True),
    )
    x_float = hidden_in.astype(jnp.float32)
    inv_first = lax.rsqrt(jnp.mean(x_float * x_float, axis=1, keepdims=True) + epsilon)
    unit_first = x_float * inv_first
    gain_first = attn_gain.astype(jnp.float32)
    normed_first = (unit_first * gain_first).astype(jnp.bfloat16)
    query_pre = mat_dot(normed_first, query_full) + query_bias.astype(jnp.float32)
    key_pre = mat_dot(normed_first, key_full) + key_bias.astype(jnp.float32)
    value_pre = mat_dot(normed_first, value_full) + value_bias.astype(jnp.float32)
    query_rot = rotate(query_pre.reshape(tok_rows, HEADS, HDIM), cosine, sine).astype(jnp.bfloat16)
    key_rot = (
        rotate(key_pre.reshape(tok_rows, KVH, HDIM), cosine, sine)
        .astype(jnp.bfloat16)
        .reshape(tok_rows, kv_width)
    )
    value_low = value_pre.astype(jnp.bfloat16)
    keys_row, values_row = (
        lax.all_gather(key_rot, "fsdp", axis=0, tiled=True),
        lax.all_gather(value_low, "fsdp", axis=0, tiled=True),
    )
    query_grouped = query_rot.reshape(tok_rows, KVH, group_size, HDIM)
    keys_grouped = keys_row.reshape(row_len, KVH, HDIM)
    values_grouped = values_row.reshape(row_len, KVH, HDIM)

    def masked_scores():
        raw_scores = (
            jnp.einsum(
                "tgjd,rgd->gjtr", query_grouped, keys_grouped, preferred_element_type=jnp.float32
            )
            * score_scale
        )
        return jnp.where(allowed[None, None], raw_scores, -1e30)

    scores = masked_scores()
    row_peak = jnp.max(scores, axis=3, keepdims=True)
    expo_vals = jnp.exp(scores - row_peak)
    row_total = jnp.sum(expo_vals, axis=3, keepdims=True)
    soft_probs = expo_vals / row_total
    log_total = row_peak + jnp.log(row_total)
    attn_heads = jnp.einsum(
        "gjtr,rgd->tgjd",
        soft_probs.astype(jnp.bfloat16),
        values_grouped,
        preferred_element_type=jnp.float32,
    )
    attn_low = attn_heads.reshape(tok_rows, model_width).astype(jnp.bfloat16)
    mid_state = x_float + mat_dot(attn_low, output_full)
    inv_second = lax.rsqrt(jnp.mean(mid_state * mid_state, axis=1, keepdims=True) + epsilon)
    unit_second = mid_state * inv_second
    gain_second = mlp_gain.astype(jnp.float32)
    normed_second = (unit_second * gain_second).astype(jnp.bfloat16)
    cot_float = out_grad.astype(jnp.float32)
    pieces = (
        lax.all_gather(w_gate, "fsdp", axis=0, tiled=True),
        lax.all_gather(w_up, "fsdp", axis=0, tiled=True),
    )
    columns = normed_second
    gate_val = mat_dot(columns, pieces[0])
    up_val = mat_dot(columns, pieces[1])
    sig_gate = jax.nn.sigmoid(gate_val)
    silu_gate = gate_val * sig_gate
    act_low = (silu_gate * up_val).astype(jnp.bfloat16)
    columns = act_low
    mlp_out = mat_dot(columns, lax.all_gather(w_down, "fsdp", axis=0, tiled=True))
    d_act = dot_right_t(out_grad, lax.all_gather(w_down, "fsdp", axis=0, tiled=True))
    columns = act_low
    down_sums = lax.psum_scatter(
        dot_left_t(columns, out_grad).astype(jnp.bfloat16), "fsdp", scatter_dimension=0, tiled=True
    ).astype(jnp.float32)
    d_gate = (d_act * up_val * sig_gate * (1.0 + gate_val * (1.0 - sig_gate))).astype(jnp.bfloat16)
    d_up = (d_act * silu_gate).astype(jnp.bfloat16)
    pieces = (
        lax.all_gather(w_gate, "fsdp", axis=0, tiled=True),
        lax.all_gather(w_up, "fsdp", axis=0, tiled=True),
    )
    partial_value = dot_right_t(d_gate, pieces[0]) + dot_right_t(d_up, pieces[1])
    columns = normed_second
    mlp_sums = lax.psum_scatter(
        jnp.concatenate([dot_left_t(columns, d_gate), dot_left_t(columns, d_up)], axis=1).astype(
            jnp.bfloat16
        ),
        "fsdp",
        scatter_dimension=0,
        tiled=True,
    ).astype(jnp.float32)
    output = mid_state + mlp_out
    d_gain_second = jnp.sum(partial_value * unit_second, axis=0)
    scaled_second = partial_value * gain_second
    d_mid = cot_float + inv_second * (
        scaled_second - unit_second * jnp.mean(scaled_second * unit_second, axis=1, keepdims=True)
    )
    d_branch_low = d_mid.astype(jnp.bfloat16)
    d_attn_low = dot_right_t(d_branch_low, output_full).astype(jnp.bfloat16)
    d_attn_grouped = d_attn_low.reshape(tok_rows, KVH, group_size, HDIM)
    scores = masked_scores()
    soft_back = jnp.exp(scores - log_total)
    probs_low = soft_back.astype(jnp.bfloat16)
    prob_grad = jnp.einsum(
        "tgjd,rgd->gjtr", d_attn_grouped, values_grouped, preferred_element_type=jnp.float32
    )
    row_delta = jnp.sum(soft_back * prob_grad, axis=3, keepdims=True)
    score_grad = (soft_back * (prob_grad - row_delta)).astype(jnp.bfloat16)
    dquery_rot = (
        jnp.einsum("gjtr,rgd->tgjd", score_grad, keys_grouped, preferred_element_type=jnp.float32)
        * score_scale
    )
    dquery_low = (
        unrotate(dquery_rot.reshape(tok_rows, HEADS, HDIM), cosine, sine)
        .reshape(tok_rows, model_width)
        .astype(jnp.bfloat16)
    )
    key_grad = (
        jnp.einsum("gjtr,tgjd->rgd", score_grad, query_grouped, preferred_element_type=jnp.float32)
        * score_scale
    )
    value_grad = jnp.einsum(
        "gjtr,tgjd->rgd", probs_low, d_attn_grouped, preferred_element_type=jnp.float32
    )
    kv_sums = lax.psum_scatter(
        jnp.concatenate(
            [
                key_grad.reshape(lax.axis_size("fsdp") * tok_rows, kv_width),
                value_grad.reshape(lax.axis_size("fsdp") * tok_rows, kv_width),
            ],
            axis=1,
        ).astype(jnp.bfloat16),
        "fsdp",
        scatter_dimension=0,
        tiled=True,
    ).astype(jnp.float32)
    dkey_low = (
        unrotate(kv_sums[:, :kv_width].reshape(tok_rows, KVH, HDIM), cosine, sine)
        .reshape(tok_rows, kv_width)
        .astype(jnp.bfloat16)
    )
    dvalue_low = kv_sums[:, kv_width:].astype(jnp.bfloat16)
    d_norm_first = (
        dot_right_t(dquery_low, query_full)
        + dot_right_t(dkey_low, key_full)
        + dot_right_t(dvalue_low, value_full)
    )
    attn_sums = lax.psum_scatter(
        jnp.concatenate(
            [
                dot_left_t(normed_first, dquery_low),
                dot_left_t(normed_first, dkey_low),
                dot_left_t(normed_first, dvalue_low),
                dot_left_t(attn_low, d_branch_low),
            ],
            axis=1,
        ).astype(jnp.bfloat16),
        "fsdp",
        scatter_dimension=0,
        tiled=True,
    ).astype(jnp.float32)
    d_gain_first = jnp.sum(d_norm_first * unit_first, axis=0)
    scaled_first = d_norm_first * gain_first
    grad_input = d_mid + inv_first * (
        scaled_first - unit_first * jnp.mean(scaled_first * unit_first, axis=1, keepdims=True)
    )
    bias_query = jnp.sum(dquery_low.astype(jnp.float32), axis=0)
    bias_key = jnp.sum(dkey_low.astype(jnp.float32), axis=0)
    bias_value = jnp.sum(dvalue_low.astype(jnp.float32), axis=0)
    bias_query, bias_key, bias_value, gain_first_sum, gain_second_sum = (
        lax.psum_scatter(bias_query, "fsdp", scatter_dimension=0, tiled=True),
        lax.psum_scatter(bias_key, "fsdp", scatter_dimension=0, tiled=True),
        lax.psum_scatter(bias_value, "fsdp", scatter_dimension=0, tiled=True),
        lax.psum_scatter(d_gain_first, "fsdp", scatter_dimension=0, tiled=True),
        lax.psum_scatter(d_gain_second, "fsdp", scatter_dimension=0, tiled=True),
    )
    (
        attn_sums,
        mlp_sums,
        down_sums,
        bias_query,
        bias_key,
        bias_value,
        gain_first_sum,
        gain_second_sum,
    ) = (
        lax.psum(attn_sums.astype(jnp.bfloat16), "rep").astype(jnp.float32),
        lax.psum(mlp_sums.astype(jnp.bfloat16), "rep").astype(jnp.float32),
        lax.psum(down_sums.astype(jnp.bfloat16), "rep").astype(jnp.float32),
        lax.psum(bias_query.astype(jnp.bfloat16), "rep").astype(jnp.float32),
        lax.psum(bias_key.astype(jnp.bfloat16), "rep").astype(jnp.float32),
        lax.psum(bias_value.astype(jnp.bfloat16), "rep").astype(jnp.float32),
        lax.psum(gain_first_sum.astype(jnp.bfloat16), "rep").astype(jnp.float32),
        lax.psum(gain_second_sum.astype(jnp.bfloat16), "rep").astype(jnp.float32),
    )
    grad_query = attn_sums[:, :model_width]
    grad_key = attn_sums[:, model_width : model_width + kv_width]
    grad_value = attn_sums[:, model_width + kv_width : model_width + 2 * kv_width]
    grad_output = attn_sums[:, model_width + 2 * kv_width :]
    grad_gate = mlp_sums[:, :ff_width]
    grad_up = mlp_sums[:, ff_width:]
    return (
        output,
        grad_input,
        grad_query,
        bias_query,
        grad_key,
        bias_key,
        grad_value,
        bias_value,
        grad_output,
        gain_first_sum,
        grad_gate,
        grad_up,
        down_sums,
        gain_second_sum,
    )


def solution(mesh):
    placed = (
        P(("rep", "fsdp"), None),
        P(("rep", "fsdp"), None),
        P("rep", None),
        P("rep", None),
        P("fsdp", None),
        P("fsdp"),
        P("fsdp", None),
        P("fsdp"),
        P("fsdp", None),
        P("fsdp"),
        P("fsdp", None),
        P("fsdp"),
        P("fsdp", None),
        P("fsdp", None),
        P("fsdp", None),
        P("fsdp"),
    )
    return jax.shard_map(
        local,
        mesh=mesh,
        in_specs=placed,
        out_specs=(
            P(("rep", "fsdp"), None),
            P(("rep", "fsdp"), None),
            P("fsdp", None),
            P("fsdp"),
            P("fsdp", None),
            P("fsdp"),
            P("fsdp", None),
            P("fsdp"),
            P("fsdp", None),
            P("fsdp"),
            P("fsdp", None),
            P("fsdp", None),
            P("fsdp", None),
            P("fsdp"),
        ),
        check_vma=False,
    )
```

profile of v0, /device:TPU:0, one launch (start us, length us, event | category | flops | bytes accessed | tf_op | source)
XLA Modules:
  0.0 2377.3 jit_solution(16772693715200293686)
XLA Ops:
  49.7 18.5 all_gather.49
  71.6 12.9 all_gather.51
  85.5 15.4 all_gather.46
  151.1 242.1 %all-gather.15.cloned.1.call-done = bf16[1536,8960]{1,0:T(8,128)(2,1)} async-done(((bf16[384,8960]{1,0:T(8,128)(2,1)}), bf16[1536,8960]{1,0:T(8,128)(2,1)}) %all-gather.15.cloned.1.call-update) | async-done | bytes 27525136 | tf_op jit(solution)/shard_map/all_gather | solution.py:179
  393.2 17.3 fusion.71
  410.5 231.5 %all-gather.13.cloned.1.call-done = bf16[1536,8960]{1,0:T(8,128)(2,1)} async-done(((bf16[384,8960]{1,0:T(8,128)(2,1)}), bf16[1536,8960]{1,0:T(8,128)(2,1)}) %all-gather.13.cloned.1.call-update) | async-done | bytes 27525136 | tf_op jit(solution)/shard_map/all_gather | solution.py:178
  642.1 17.7 fusion.70
  659.8 231.2 %all-gather.17.cloned.1.call-done = bf16[8960,1536]{1,0:T(8,128)(2,1)} async-done(((bf16[2240,1536]{1,0:T(8,128)(2,1)}), bf16[8960,1536]{1,0:T(8,128)(2,1)}) %all-gather.17.cloned.1.call-update) | async-done | bytes 27525136 | tf_op jit(solution)/shard_map/all_gather | solution.py:188
  890.9 24.7 %multiply_convert_fusion = (bf16[320,8960]{1,0:T(8,128)(2,1)}, bf16[320,8960]{1,0:T(8,128)(2,1)}, bf16[320,8960]{1,0:T(8,128)(2,1)}) fusion(f32[320,8960]{1,0:T(8,128)} %fusion.70, f32[320,8960]{1,0:T(8,128)} %fusion.71, bf16[320,1536]{1,0:T(8,128)(2,1)S(1)} %copy-done.33, bf16[8960,1536]{1,0:T(8,128)(2,1)} %all-gather.17.cloned.1.call-done), kind=kOutput, calls=%fused_computation.15 | convolution fusion | flops 8851046400 | bytes 68648960 | tf_op jit(solution)/shard_map/dot_general | solution.py:60
  915.7 16.5 fusion.72
  932.1 17.3 multiply_reduce_fusion
  976.8 13.4 fusion.2
  1039.9 14.6 copy.143
  1054.6 22.4 convolution_convert_fusion.2
  1077.1 21.5 convolution_convert_fusion
  1098.6 21.1 convolution_convert_fusion.1
  1119.7 37.6 %pad_maximum_fusion = bf16[1536,17920]{1,0:T(8,128)(2,1)} fusion(bf16[1536,8960]{1,0:T(8,128)(2,1)} %convolution_convert_fusion, bf16[1536,8960]{1,0:T(8,128)(2,1)} %convolution_convert_fusion.1), kind=kLoop, calls=%fused_computation | loop fusion | flops 110100480 | bytes 110100480 | tf_op jit(solution)/shard_map/concatenate | solution.py:203
  1167.1 239.5 %reduce-scatter.11.cloned.1.call-done = bf16[2240,1536]{1,0:T(8,128)(2,1)} async-done(((bf16[8960,1536]{1,0:T(8,128)(2,1)}), bf16[2240,1536]{1,0:T(8,128)(2,1)}) %reduce-scatter.11.cloned.1.call-update) | async-done | bytes 6881296 | tf_op jit(solution)/shard_map/reduce_scatter | solution.py:191
  1406.6 465.6 %reduce-scatter.9.cloned.1.call-done = bf16[384,17920]{1,0:T(8,128)(2,1)} async-done(((bf16[1536,17920]{1,0:T(8,128)(2,1)}), bf16[384,17920]{1,0:T(8,128)(2,1)}) %reduce-scatter.9.cloned.1.call-update) | async-done | bytes 13762576 | tf_op jit(solution)/shard_map/reduce_scatter | solution.py:202
  1885.8 16.9 convolution_add_fusion.3
  1906.0 15.9 all-reduce.7
  1922.3 14.6 all-reduce.8
  1943.1 392.3 %all-reduce.13.cloned.1.call-done = (bf16[384,3584]{0,1:T(8,128)(2,1)}, bf16[384,17920]{1,0:T(8,128)(2,1)}, bf16[2240,1536]{1,0:T(8,128)(2,1)}) async-done(((bf16[384,3584]{0,1:T(8,128)(2,1)}, bf16[384,17920]{1,0:T(8,128)(2,1)}, bf16[2240,1536]{1,0:T(8,128)(2,1)}), (bf16[384,3584]{0,1:T(8,128)(2,1)}, bf16[384,17920]{1,0:T(8,128)(2,1)}, bf16[2240,1536]{1,0:T(8,128)(2,1)})) %all-reduce.13.cloned.1.call-update) | async-done | bytes 23396368 | tf_op jit(solution)/shard_map/psum | solution.py:305
  2356.7 13.6 fusion.63
  (254 shorter events, 226.0 us)
Async XLA Ops:
  7.2 110.5 %all-gather.9.cloned.1.call-start = ((), (), s32[]{:S(2)}) async-start(), calls=%async_computation.4 | async-start | bytes 5898240 | tf_op jit(solution)/shard_map/all_gather | solution.py:116
  7.9 138.4 %all-gather.11.cloned.1.call-start = ((), (), s32[]{:S(2)}) async-start(), calls=%async_computation.5 | async-start | bytes 5898240 | tf_op jit(solution)/shard_map/all_gather | solution.py:119
  8.7 384.5 %all-gather.15.cloned.1.call-start = ((), (), s32[]{:S(2)}) async-start(), calls=%async_computation.7 | async-start | bytes 34406400 | tf_op jit(solution)/shard_map/all_gather | solution.py:179
  9.4 632.7 %all-gather.13.cloned.1.call-start = ((), (), s32[]{:S(2)}) async-start(), calls=%async_computation.6 | async-start | bytes 34406400 | tf_op jit(solution)/shard_map/all_gather | solution.py:178
  10.0 37.0 %copy-start.52 = (s32[1,8]{1,0:T(1,128)S(1)}, s32[1,8]{1,0:T(1,128)}, u32[]{:S(2)}) copy-start(s32[1,8]{1,0:T(1,128)} %param.18) | copy-start | bytes 100
  10.1 39.6 %copy-start.37 = (bf16[384,256]{1,0:T(8,128)(2,1)S(1)}, bf16[384,256]{1,0:T(8,128)(2,1)}, u32[]{:S(2)}) copy-start(bf16[384,256]{1,0:T(8,128)(2,1)} %param.22) | copy-start | bytes 589828
  10.1 880.9 %all-gather.17.cloned.1.call-start = ((), (), s32[]{:S(2)}) async-start(), calls=%async_computation.8 | async-start | bytes 34406400 | tf_op jit(solution)/shard_map/all_gather | solution.py:188
  10.6 57.6 %copy-start.4 = (bf16[320,1536]{1,0:T(8,128)(2,1)S(1)}, bf16[320,1536]{1,0:T(8,128)(2,1)}, u32[]{:S(2)}) copy-start(bf16[320,1536]{1,0:T(8,128)(2,1)} %param.16) | copy-start | bytes 2949124
  10.7 1014.4 %reduce-scatter.7.cloned.1.call-start = ((), (), s32[]{:S(2)}) async-start(), calls=%async_computation.9 | async-start | bytes 1638400 | tf_op jit(solution)/shard_map/reduce_scatter | solution.py:243
  39.1 78.5 %copy-start.39 = (f32[1536]{0:T(1024)}, f32[1536]{0:T(1024)S(1)}, u32[]{:S(2)}) copy-start(f32[1536]{0:T(1024)S(1)} %reshape.339) | copy-start | bytes 18436
  48.7 21.5 copy-start.23
  48.9 76.8 %copy-start.26 = (f32[320,128]{0,1:T(8,128)}, f32[320,128]{0,1:T(8,128)S(1)}, u32[]{:S(2)}) copy-start(f32[320,128]{0,1:T(8,128)S(1)} %copy.98) | copy-start | bytes 491524
  69.2 48.5 %copy-start.41 = (f32[320]{0:T(512)}, f32[320]{0:T(512)S(1)}, u32[]{:S(2)}) copy-start(f32[320]{0:T(512)S(1)} %add_rsqrt_fusion.1) | copy-start | bytes 3844
  150.8 798.6 %copy-start.2 = (f32[320,1536]{1,0:T(8,128)}, f32[320,1536]{1,0:T(8,128)S(1)}, u32[]{:S(2)}) copy-start(f32[320,1536]{1,0:T(8,128)S(1)} %get-tuple-element.119) | copy-start | bytes 5898244
  151.1 242.1 %copy-start.34 = (bf16[320,1536]{1,0:T(8,128)(2,1)}, bf16[320,1536]{1,0:T(8,128)(2,1)S(1)}, u32[]{:S(2)}) copy-start(bf16[320,1536]{1,0:T(8,128)(2,1)S(1)} %multiply_convert_fusion.3) | copy-start | bytes 2949124
  410.5 480.4 %copy-start.33 = (bf16[320,1536]{1,0:T(8,128)(2,1)S(1)}, bf16[320,1536]{1,0:T(8,128)(2,1)}, u32[]{:S(2)}) copy-start(bf16[320,1536]{1,0:T(8,128)(2,1)} %param.17) | copy-start | bytes 2949124
  915.7 37.1 %slice-start = ((s8[4718592]{0:T(1024)(128)(4,1)}), s8[4194304]{0:T(1024)(128)(4,1)S(1)}, s32[]{:S(2)}) async-start(s8[4718592]{0:T(1024)(128)(4,1)} %bitcast.131), calls=%async_computation.14 | async-start | bytes 8388608
  932.1 20.7 slice-start.1
  995.5 166.9 %reduce-scatter.13.cloned.1.call-start = ((), (), s32[]{:S(2)}) async-start(), calls=%async_computation.12 | async-start | bytes 13762560
  1054.5 352.1 %reduce-scatter.11.cloned.1.call-start = ((), (), s32[]{:S(2)}) async-start(), calls=%async_computation.11 | async-start | bytes 34406400 | tf_op jit(solution)/shard_map/reduce_scatter | solution.py:191
  1077.0 795.2 %reduce-scatter.9.cloned.1.call-start = ((), (), s32[]{:S(2)}) async-start(), calls=%async_computation.10 | async-start | bytes 68812800 | tf_op jit(solution)/shard_map/reduce_scatter | solution.py:202
  1077.1 21.5 copy-start.35
  1157.3 1178.1 %all-reduce.13.cloned.1.call-start = ((), (), s32[]{:S(2)}) async-start(), calls=%async_computation.13 | async-start | bytes 46792704 | tf_op jit(solution)/shard_map/psum | solution.py:305
  1904.0 35.7 %copy-start.10 = (f32[320,1536]{1,0:T(8,128)S(1)}, f32[320,1536]{1,0:T(8,128)}, u32[]{:S(2)}) copy-start(f32[320,1536]{1,0:T(8,128)} %copy-done.8) | copy-start | bytes 5898244
  (43 other events, 213.6 us)
Sparse Core Ops, SparseCore 0:
  9.9 69.6 all-gather.8
  81.4 62.6 all-gather.10
  146.0 247.1 all-gather.14
  394.9 247.1 all-gather.12
  643.8 247.1 all-gather.16
  995.6 29.3 reduce-scatter.6
  1054.6 107.7 reduce-scatter.12
  1165.5 240.9 reduce-scatter.10
  1410.0 462.1 reduce-scatter.8
  1875.5 459.8 all-reduce.12
where the time goes:
time: 2380 us
  waiting for transfers between devices  1810 us (76%)
  matrix products  247 us (10%)
  blocking collectives  124 us (5%)
  other arithmetic  96 us (4%)
  local copies, waits for them, and re-layouts  78.8 us (3%)
    reduce_scatter x1, waiting for transfers between devices, local(): lax.psum_scatter(jnp.concatenate([dot_left_t(columns, d_gate), dot_left_t...  466 us
    psum x1, waiting for transfers between devices, local(): lax.psum(attn_sums.astype(jnp.bfloat16), 'rep').astype(jnp.float32)  392 us
    all_gather x1, waiting for transfers between devices, local(): lax.all_gather(w_up, 'fsdp', axis=0, tiled=True)  242 us
    reduce_scatter x1, waiting for transfers between devices, local(): lax.psum_scatter(dot_left_t(columns, out_grad).astype(jnp.bfloat16), 'fsd...  239 us
    all_gather x1, waiting for transfers between devices, local(): lax.all_gather(w_gate, 'fsdp', axis=0, tiled=True)  232 us
    all_gather x1, waiting for transfers between devices, local(): lax.all_gather(w_down, 'fsdp', axis=0, tiled=True)  231 us
    dot_general x7, matrix products, dot_left_t(): lax.dot_general(left, right, (((0,), (0,)), ((), ())), preferred_element_...  76.4 us
    dot_general x7, matrix products, dot_right_t(): lax.dot_general(left, right, (((1,), (1,)), ((), ())), preferred_element_...  67.8 us
  transfers between devices with their start and end apart: 10, of which 8 were waited for; matrix products, arithmetic and copies ran while one was open for 10% of the time, Pallas kernels for 0%

commit v1 on v0

--- a/solution.py
+++ b/solution.py
@@ -9,6 +9,12 @@
 PIECE = 256
 epsilon = 1e-06
 rope_base = 1000000.0
+
+
+def gather_and_add(array, axis):
+    terms = lax.all_gather(array, axis, axis=0, tiled=False)
+    result = terms.sum(axis=0)
+    return result
 
 
 def row_layout(positions, lengths, starts, piece_len):
@@ -302,7 +308,7 @@
         gain_first_sum,
         gain_second_sum,
     ) = (
-        lax.psum(attn_sums.astype(jnp.bfloat16), "rep").astype(jnp.float32),
+        gather_and_add(attn_sums.astype(jnp.bfloat16), "rep").astype(jnp.float32),
         lax.psum(mlp_sums.astype(jnp.bfloat16), "rep").astype(jnp.float32),
         lax.psum(down_sums.astype(jnp.bfloat16), "rep").astype(jnp.float32),
         lax.psum(bias_query.astype(jnp.bfloat16), "rep").astype(jnp.float32),

time: 2380 us -> 2510 us (1.055)
  waiting for transfers between devices: 1810 us -> 1900 us
    all_gather x0 -> x1, waiting for transfers between devices: none -> 124 us  [gather_and_add(): terms = lax.all_gather(array, axis, axis=0, tiled=False)]
    psum x1, waiting for transfers between devices: 392 us -> 354 us  [local(): lax.psum(mlp_sums.astype(jnp.bfloat16), 'rep').astype(jnp.float32)]
    unnamed x133 -> x138, local copies, waits for them, and re-layouts: 41.4 us -> 62.5 us
  transfers between devices with their start and end apart: 10 -> 11, of which waited for: 8 -> 9; matrix products, arithmetic and copies ran while one was open for 10% -> 12% of each run, Pallas kernels for 0% -> 0%
where the time goes in v1:
time: 2510 us; the launch traced here: 2500 us
  waiting for transfers between devices  1900 us (76%)
  matrix products  249 us (10%)
  blocking collectives  124 us (5%)
  other arithmetic  119 us (5%)
  local copies, waits for them, and re-layouts  94.3 us (4%)
    reduce_scatter x1, waiting for transfers between devices, local(): lax.psum_scatter(jnp.concatenate([dot_left_t(columns, d_gate), dot_left_t...  466 us
    psum x1, waiting for transfers between devices, local(): lax.psum(mlp_sums.astype(jnp.bfloat16), 'rep').astype(jnp.float32)  354 us
    all_gather x1, waiting for transfers between devices, local(): lax.all_gather(w_up, 'fsdp', axis=0, tiled=True)  242 us
    reduce_scatter x1, waiting for transfers between devices, local(): lax.psum_scatter(dot_left_t(columns, out_grad).astype(jnp.bfloat16), 'fsd...  239 us
    all_gather x1, waiting for transfers between devices, local(): lax.all_gather(w_gate, 'fsdp', axis=0, tiled=True)  231 us
    all_gather x1, waiting for transfers between devices, local(): lax.all_gather(w_down, 'fsdp', axis=0, tiled=True)  231 us
    all_gather x1, waiting for transfers between devices, gather_and_add(): terms = lax.all_gather(array, axis, axis=0, tiled=False)  124 us
    dot_general x7, matrix products, dot_left_t(): lax.dot_general(left, right, (((0,), (0,)), ((), ())), preferred_element_...  76.4 us
  transfers between devices with their start and end apart: 11, of which 9 were waited for; matrix products, arithmetic and copies ran while one was open for 12% of the time, Pallas kernels for 0%

profile of v1, /device:TPU:0, one launch (start us, length us, event | category | flops | bytes accessed | tf_op | source)
XLA Modules:
  0.0 2503.5 jit_solution(17073849545628568223)
XLA Ops:
  49.7 18.5 all_gather.55
  85.5 15.4 all_gather.52
  151.2 242.0 %all-gather.17.cloned.1.call-done = bf16[1536,8960]{1,0:T(8,128)(2,1)} async-done(((bf16[384,8960]{1,0:T(8,128)(2,1)}), bf16[1536,8960]{1,0:T(8,128)(2,1)}) %all-gather.17.cloned.1.call-update) | async-done | bytes 27525136 | tf_op jit(solution)/shard_map/all_gather | solution.py:185
  393.2 17.4 fusion.71
  410.6 231.5 %all-gather.15.cloned.1.call-done = bf16[1536,8960]{1,0:T(8,128)(2,1)} async-done(((bf16[384,8960]{1,0:T(8,128)(2,1)}), bf16[1536,8960]{1,0:T(8,128)(2,1)}) %all-gather.15.cloned.1.call-update) | async-done | bytes 27525136 | tf_op jit(solution)/shard_map/all_gather | solution.py:184
  642.1 17.7 fusion.70
  659.8 231.2 %all-gather.19.cloned.1.call-done = bf16[8960,1536]{1,0:T(8,128)(2,1)} async-done(((bf16[2240,1536]{1,0:T(8,128)(2,1)}), bf16[8960,1536]{1,0:T(8,128)(2,1)}) %all-gather.19.cloned.1.call-update) | async-done | bytes 27525136 | tf_op jit(solution)/shard_map/all_gather | solution.py:194
  890.9 24.7 multiply_convert_fusion
  915.6 16.4 fusion.72
  932.1 17.3 multiply_reduce_fusion
  1039.8 14.6 copy.135
  1054.5 22.5 convolution_convert_fusion.2
  1077.0 21.5 convolution_convert_fusion
  1098.5 21.1 convolution_convert_fusion.1
  1119.6 37.6 %pad_maximum_fusion = bf16[1536,17920]{1,0:T(8,128)(2,1)} fusion(bf16[1536,8960]{1,0:T(8,128)(2,1)} %convolution_convert_fusion, bf16[1536,8960]{1,0:T(8,128)(2,1)} %convolution_convert_fusion.1), kind=kLoop, calls=%fused_computation | loop fusion | flops 110100480 | bytes 110100480 | tf_op jit(solution)/shard_map/concatenate | solution.py:209
  1167.2 239.4 %reduce-scatter.11.cloned.1.call-done = bf16[2240,1536]{1,0:T(8,128)(2,1)} async-done(((bf16[8960,1536]{1,0:T(8,128)(2,1)}), bf16[2240,1536]{1,0:T(8,128)(2,1)}) %reduce-scatter.11.cloned.1.call-update) | async-done | bytes 6881296 | tf_op jit(solution)/shard_map/reduce_scatter | solution.py:197
  1406.5 465.6 %reduce-scatter.9.cloned.1.call-done = bf16[384,17920]{1,0:T(8,128)(2,1)} async-done(((bf16[1536,17920]{1,0:T(8,128)(2,1)}), bf16[384,17920]{1,0:T(8,128)(2,1)}) %reduce-scatter.9.cloned.1.call-update) | async-done | bytes 13762576 | tf_op jit(solution)/shard_map/reduce_scatter | solution.py:208
  1886.0 18.2 convolution_add_fusion.3
  1907.5 15.8 all-reduce.7
  1923.6 15.1 all-reduce.8
  1944.8 123.6 %all-gather.21.cloned.1.call-done = bf16[3072,3584]{0,1:T(8,128)(2,1)} async-done(((bf16[384,3584]{0,1:T(8,128)(2,1)}), bf16[3072,3584]{0,1:T(8,128)(2,1)}) %all-gather.21.cloned.1.call-update) | async-done | bytes 22020112 | tf_op jit(solution)/shard_map/all_gather | solution.py:15
  2068.4 21.2 copy.140
  2089.6 23.0 bitcast_reduce_fusion
  2122.1 354.3 %all-reduce.13.cloned.1.call-done = (bf16[384,17920]{1,0:T(8,128)(2,1)}, bf16[2240,1536]{1,0:T(8,128)(2,1)}) async-done(((bf16[384,17920]{1,0:T(8,128)(2,1)}, bf16[2240,1536]{1,0:T(8,128)(2,1)}), (bf16[384,17920]{1,0:T(8,128)(2,1)}, bf16[2240,1536]{1,0:T(8,128)(2,1)})) %all-reduce.13.cloned.1.call-update) | async-done | bytes 20643856 | tf_op jit(solution)/shard_map/psum | solution.py:312
  (263 shorter events, 261.2 us)
Async XLA Ops:
  7.2 110.5 %all-gather.11.cloned.1.call-start = ((), (), s32[]{:S(2)}) async-start(), calls=%async_computation.4 | async-start | bytes 5898240 | tf_op jit(solution)/shard_map/all_gather | solution.py:122
  7.9 138.5 %all-gather.13.cloned.1.call-start = ((), (), s32[]{:S(2)}) async-start(), calls=%async_computation.5 | async-start | bytes 5898240 | tf_op jit(solution)/shard_map/all_gather | solution.py:125
  8.7 384.5 %all-gather.17.cloned.1.call-start = ((), (), s32[]{:S(2)}) async-start(), calls=%async_computation.7 | async-start | bytes 34406400 | tf_op jit(solution)/shard_map/all_gather | solution.py:185
  9.4 632.7 %all-gather.15.cloned.1.call-start = ((), (), s32[]{:S(2)}) async-start(), calls=%async_computation.6 | async-start | bytes 34406400 | tf_op jit(solution)/shard_map/all_gather | solution.py:184
  10.0 37.0 %copy-start.54 = (s32[1,8]{1,0:T(1,128)S(1)}, s32[1,8]{1,0:T(1,128)}, u32[]{:S(2)}) copy-start(s32[1,8]{1,0:T(1,128)} %param.18) | copy-start | bytes 100
  10.1 39.7 %copy-start.39 = (bf16[384,256]{1,0:T(8,128)(2,1)S(1)}, bf16[384,256]{1,0:T(8,128)(2,1)}, u32[]{:S(2)}) copy-start(bf16[384,256]{1,0:T(8,128)(2,1)} %param.22) | copy-start | bytes 589828
  10.1 880.9 %all-gather.19.cloned.1.call-start = ((), (), s32[]{:S(2)}) async-start(), calls=%async_computation.8 | async-start | bytes 34406400 | tf_op jit(solution)/shard_map/all_gather | solution.py:194
  10.6 57.6 %copy-start.5 = (bf16[320,1536]{1,0:T(8,128)(2,1)S(1)}, bf16[320,1536]{1,0:T(8,128)(2,1)}, u32[]{:S(2)}) copy-start(bf16[320,1536]{1,0:T(8,128)(2,1)} %param.16) | copy-start | bytes 2949124
  10.7 1014.3 %reduce-scatter.7.cloned.1.call-start = ((), (), s32[]{:S(2)}) async-start(), calls=%async_computation.9 | async-start | bytes 1638400 | tf_op jit(solution)/shard_map/reduce_scatter | solution.py:249
  39.1 78.5 %copy-start.41 = (f32[1536]{0:T(1024)}, f32[1536]{0:T(1024)S(1)}, u32[]{:S(2)}) copy-start(f32[1536]{0:T(1024)S(1)} %reshape.340) | copy-start | bytes 18436
  48.7 21.5 copy-start.25
  48.9 76.8 %copy-start.28 = (f32[320,128]{0,1:T(8,128)}, f32[320,128]{0,1:T(8,128)S(1)}, u32[]{:S(2)}) copy-start(f32[320,128]{0,1:T(8,128)S(1)} %copy.90) | copy-start | bytes 491524
  69.2 48.5 %copy-start.43 = (f32[320]{0:T(512)}, f32[320]{0:T(512)S(1)}, u32[]{:S(2)}) copy-start(f32[320]{0:T(512)S(1)} %add_rsqrt_fusion.1) | copy-start | bytes 3844
  150.9 798.5 %copy-start.3 = (f32[320,1536]{1,0:T(8,128)}, f32[320,1536]{1,0:T(8,128)S(1)}, u32[]{:S(2)}) copy-start(f32[320,1536]{1,0:T(8,128)S(1)} %get-tuple-element.90) | copy-start | bytes 5898244
  151.2 242.0 %copy-start.36 = (bf16[320,1536]{1,0:T(8,128)(2,1)}, bf16[320,1536]{1,0:T(8,128)(2,1)S(1)}, u32[]{:S(2)}) copy-start(bf16[320,1536]{1,0:T(8,128)(2,1)S(1)} %multiply_convert_fusion.3) | copy-start | bytes 2949124
  410.6 480.4 %copy-start.35 = (bf16[320,1536]{1,0:T(8,128)(2,1)S(1)}, bf16[320,1536]{1,0:T(8,128)(2,1)}, u32[]{:S(2)}) copy-start(bf16[320,1536]{1,0:T(8,128)(2,1)} %param.17) | copy-start | bytes 2949124
  915.6 37.1 %slice-start = ((s8[4718592]{0:T(1024)(128)(4,1)}), s8[4194304]{0:T(1024)(128)(4,1)S(1)}, s32[]{:S(2)}) async-start(s8[4718592]{0:T(1024)(128)(4,1)} %bitcast.137), calls=%async_computation.15 | async-start | bytes 8388608
  995.5 166.9 %reduce-scatter.13.cloned.1.call-start = ((), (), s32[]{:S(2)}) async-start(), calls=%async_computation.13 | async-start | bytes 13762560
  1054.4 352.1 %reduce-scatter.11.cloned.1.call-start = ((), (), s32[]{:S(2)}) async-start(), calls=%async_computation.11 | async-start | bytes 34406400 | tf_op jit(solution)/shard_map/reduce_scatter | solution.py:197
  1076.9 795.2 %reduce-scatter.9.cloned.1.call-start = ((), (), s32[]{:S(2)}) async-start(), calls=%async_computation.10 | async-start | bytes 68812800 | tf_op jit(solution)/shard_map/reduce_scatter | solution.py:208
  1077.0 21.5 copy-start.37
  1157.2 911.2 %all-gather.21.cloned.1.call-start = ((), (), s32[]{:S(2)}) async-start(), calls=%async_computation.12 | async-start | bytes 24772608 | tf_op jit(solution)/shard_map/all_gather | solution.py:15
  1166.9 1309.5 %all-reduce.13.cloned.1.call-start = ((), (), s32[]{:S(2)}) async-start(), calls=%async_computation.14 | async-start | bytes 41287680 | tf_op jit(solution)/shard_map/psum | solution.py:312
  1905.4 36.0 %copy-start.12 = (f32[320,1536]{1,0:T(8,128)S(1)}, f32[320,1536]{1,0:T(8,128)}, u32[]{:S(2)}) copy-start(f32[320,1536]{1,0:T(8,128)} %copy-done.10) | copy-start | bytes 5898244
  (46 other events, 249.5 us)
Sparse Core Ops, SparseCore 0:
  9.9 69.6 all-gather.10
  81.4 62.6 all-gather.12
  146.0 247.1 all-gather.16
  394.9 247.1 all-gather.14
  643.8 247.1 all-gather.18
  995.6 29.3 reduce-scatter.6
  1054.5 107.8 reduce-scatter.12
  1165.5 240.9 reduce-scatter.10
  1409.9 462.1 reduce-scatter.8
  1874.2 194.1 all-gather.20
  2071.0 405.2 all-reduce.12
